TPU v7x, 128 devices: a whole 4x4x4 slice. The times are simulated.
128 devices in a mesh: blk: 32 (over z, x, core), nb: 4 (over y).
Axes of the slice: x: 4, y: 4, z: 4, core: 2. Of those that a mesh axis runs over, the one named last changes fastest.
Arguments:
- latent: float32 [1024, 96, 128], P(('blk', 'nb')), may hold values from -8 to 8
- coords: float32 [1024, 2, 128], P(('blk', 'nb')), may hold values from 0 to 1
- labels: int32 [1024, 96, 128], P(('blk', 'nb')), may hold values 0 or 1
- owner: int32 [1024, 4], P(('blk', 'nb')), may hold values from 0 to 127, all different within a row; in each aligned block of 8 rows (0 to 7, 8 to 15, ...) at most 2 rows name the same one
- slot: int32 [1024, 4], P(('blk', 'nb')), may hold values from 0 to 7
Outputs:
- new_latent: float32 [1024, 96, 128], P(('blk', 'nb'))
- step_rms: float32 [96], replicated
Inputs may be any that keep to these rules, and one draw needn't show every extreme that they name: The 4 owners of one block are distinct; the 8 blocks stored on one device name any one owner at most 2 times.
All inputs are finite; a program needn't handle non-finite values. No bound on the sum of `labels` on one device may be relied on, other than what follows from the above.
Results may differ from a plain program's by a relative error of at most 0.0003.
Values sent between devices are 32-bit elements; how exact they have to be, the bound alone decides.
A program may use at most 192 MiB of HBM per device.

v0:
```python
import math
import functools
import jax
import jax.numpy as jnp
from jax import lax
from jax.experimental import pallas as pl
from jax.experimental.pallas import tpu as pltpu
from jax.sharding import PartitionSpec as P

nugget = 0.25
length_scale = 0.1
NN = (((1,), (0,)), ((), ()))
NT = (((1,), (1,)), ((), ()))
TN = (((0,), (0,)), ((), ()))


def split(x):
    high = x.astype(jnp.bfloat16)
    return high, (x - high.astype(jnp.float32)).astype(jnp.bfloat16)


def dot(a, b, dims):
    return lax.dot_general(a, b, dims, preferred_element_type=jnp.float32)


def wide(a, b, dims=NN):
    ca, cb = dims[0][0][0], dims[0][1][0]
    left = jnp.concatenate([a[0], a[1], a[0]], axis=ca)
    right = jnp.concatenate([b[0], b[0], b[1]], axis=cb)
    return dot(left, right, dims)


def small(a, b, dims=NN):
    return dot(a[0], b[0], dims) + (dot(a[0], b[1], dims) + dot(a[1], b[0], dims))


def eliminate(packs):
    lane = lax.broadcasted_iota(jnp.int32, (8, 128), 1)
    row = lax.broadcasted_iota(jnp.int32, (8, 128), 0)
    base = lane & 64
    inner = lane & 63

    def pick(x, at):
        return jnp.take_along_axis(x, at, axis=1)

    for top in range(8):
        def step(t, carry, top=top):
            sub = 2 * t
            p = 8 * top + sub
            at0 = base + p
            at1 = at0 + 1
            first, second = inner == p, inner == p + 1
            own = first | second
            r1 = [jnp.broadcast_to(pack[pl.ds(p, 1), :], (8, 128)) for pack in packs]
            r2 = [jnp.broadcast_to(pack[pl.ds(p + 1, 1), :], (8, 128)) for pack in packs]
            tiles = [[pack[8 * s:8 * s + 8, :] for s in range(top, 8)] for pack in packs]
            a = [pick(x, at0) for x in r1]
            c1 = [[pick(y, at0) for y in ys] for ys in tiles]
            b = [pick(x, at1) for x in r1]
            d = [pick(x, at1) for x in r2]
            c2 = [[pick(y, at1) for y in ys] for ys in tiles]
            for q, pack in enumerate(packs):
                det = a[q] * d[q] - b[q] * b[q]
                rdet = 1.0 / det
                e1 = jnp.where(first, 1.0, jnp.where(second, 0.0, r1[q]))
                e2 = jnp.where(first, 0.0, jnp.where(second, 1.0, r2[q]))
                new1 = (d[q] * e1 - b[q] * e2) * rdet
                new2 = (a[q] * e2 - b[q] * e1) * rdet
                ra = lax.rsqrt(a[q])
                done1 = e1 * ra
                done2 = new2 * (det * (ra * lax.rsqrt(det)))
                for i, y in enumerate(tiles[q]):
                    x = jnp.where(own, 0.0, y) - c1[q][i] * new1 - c2[q][i] * new2
                    if i == 0:
                        x = jnp.where(row > sub + 1, x, jnp.where(row == sub, done1, jnp.where(row == sub + 1, done2, y)))
                    pack[8 * (top + i):8 * (top + i) + 8, :] = x
            return carry

        lax.fori_loop(0, 4, step, 0)


def lower64(x):
    keep = lax.broadcasted_iota(jnp.int32, (64, 64), 0) >= lax.broadcasted_iota(jnp.int32, (64, 64), 1)
    return jnp.where(keep, x, 0.0)


def factor_kernel(owner_ref, slot_ref, coords_ref, own_ref, gh_ref, gl_ref, lh_ref, ll_ref, qd_ref, cov, wh, wl, linv, *packs):
    n = own_ref.shape[0]
    near = owner_ref.shape[1]
    nt = near + 1
    last = near * 128
    scale = math.sqrt(3.0) / length_scale

    def build(m, carry):
        pts = [
            [coords_ref[owner_ref[m, k], pl.ds(2 * slot_ref[m, k] + i, 1), :] * scale for i in range(2)]
            for k in range(near)
        ] + [[own_ref[m, i:i + 1] * scale for i in range(2)]]
        for i in range(nt):
            xc = jnp.broadcast_to(pts[i][0], (128, 128)).T
            yc = jnp.broadcast_to(pts[i][1], (128, 128)).T
            for j in range(i + 1):
                dx = xc - pts[j][0]
                dy = yc - pts[j][1]
                q = dx * dx + dy * dy
                s = q * lax.rsqrt(jnp.maximum(q, 1e-30))
                c = (1.0 + s) * jnp.exp(-s)
                if i == j:
                    diag = lax.broadcasted_iota(jnp.int32, (128, 128), 0) == lax.broadcasted_iota(
                        jnp.int32, (128, 128), 1
                    )
                    c = c + jnp.where(diag, nugget, 0.0)
                cov[m, i * 128:(i + 1) * 128, j * 128:(j + 1) * 128] = c
        return carry

    lax.fori_loop(0, n, build, 0)

    def terms(ref_h, ref_l, *at):
        return ref_h[at], ref_l[at]

    for j in range(nt):
        lo, hi = j * 128, (j + 1) * 128
        rows = slice(lo, hi)

        if j:
            def left(m, carry):
                a = (wh[m, lo:, :lo], wl[m, lo:, :lo])
                b = (wh[m, lo:hi, :lo], wl[m, lo:hi, :lo])
                cov[m, lo:, lo:hi] = cov[m, lo:, lo:hi] - wide(a, b, NT)
                return carry

            lax.fori_loop(0, n, left, 0)

        for m in range(n):
            packs[m // 2][:, (m % 2) * 64:(m % 2) * 64 + 64] = cov[m, lo:lo + 64, lo:lo + 64]
        eliminate(packs)
        for m in range(n):
            at = (m % 2) * 64
            top = split(lower64(packs[m // 2][:, at:at + 64]))
            w = split(small(split(cov[m, lo + 64:hi, lo:lo + 64]), top, NT))
            linv[j, m, 0:64, 0:64] = top[0].astype(jnp.float32) + top[1].astype(jnp.float32)
            linv[j, m, 0:64, 64:128] = jnp.zeros((64, 64), jnp.float32)
            linv[j, m, 64:128, 0:64] = small(w, top)
            linv[j, m, 64:128, 64:128] = cov[m, lo + 64:hi, lo + 64:hi] - small(w, w, NT)
        for m in range(n):
            packs[m // 2][:, (m % 2) * 64:(m % 2) * 64 + 64] = linv[j, m, 64:128, 64:128]
        eliminate(packs)
        for m in range(n):
            at = (m % 2) * 64
            low = lower64(packs[m // 2][:, at:at + 64])
            linv[j, m, 64:128, 64:128] = low
            linv[j, m, 64:128, 0:64] = -small(split(low), split(linv[j, m, 64:128, 0:64]))

        if j < near:
            def panel(m, carry):
                w = split(wide(split(cov[m, hi:, lo:hi]), split(linv[j, m]), NT))
                wh[m, hi:, lo:hi] = w[0]
                wl[m, hi:, lo:hi] = w[1]
                return carry

            lax.fori_loop(0, n, panel, 0)

    def back(m, carry):
        for k in reversed(range(near)):
            lo, hi = k * 128, (k + 1) * 128
            g = wh[m, last:, lo:hi].astype(jnp.float32) + wl[m, last:, lo:hi].astype(jnp.float32)
            if hi < last:
                g = g - wide((gh_ref[m, :, hi:last], gl_ref[m, :, hi:last]), (wh[m, hi:last, lo:hi], wl[m, hi:last, lo:hi]))
            gh_ref[m, :, lo:hi], gl_ref[m, :, lo:hi] = split(wide(split(g), split(linv[k, m])))
        li = linv[near, m]
        lh_ref[m], ll_ref[m] = split(li)
        qd_ref[m] = jnp.sum(li * li, axis=0, keepdims=True)
        return carry

    lax.fori_loop(0, n, back, 0)


def factor(owner, slot, coords_all, coords_own):
    n, near = owner.shape
    width = (near + 1) * 128
    return pl.pallas_call(
        factor_kernel,
        out_shape=(jax.ShapeDtypeStruct((n, 128, near * 128), jnp.bfloat16),) * 2
        + (jax.ShapeDtypeStruct((n, 128, 128), jnp.bfloat16),) * 2
        + (jax.ShapeDtypeStruct((n, 1, 128), jnp.float32),),
        in_specs=[pl.BlockSpec(memory_space=pltpu.SMEM)] * 2 + [pl.BlockSpec(memory_space=pltpu.VMEM)] * 2,
        out_specs=(pl.BlockSpec(memory_space=pltpu.VMEM),) * 5,
        scratch_shapes=[
            pltpu.VMEM((n, width, width), jnp.float32),
            pltpu.VMEM((n, width, width - 128), jnp.bfloat16),
            pltpu.VMEM((n, width, width - 128), jnp.bfloat16),
            pltpu.VMEM((near + 1, n, 128, 128), jnp.float32),
        ]
        + [pltpu.VMEM((64, 128), jnp.float32)] * (n // 2),
        compiler_params=pltpu.CompilerParams(vmem_limit_bytes=56 * 1024 * 1024),
        cost_estimate=pl.CostEstimate(flops=2_000_000_000, bytes_accessed=5_000_000, transcendentals=4_000_000),
        name="factor",
    )(owner, slot, coords_all, coords_own)


MESH = pl.DeviceIdType.MESH
SIDE = 4
ROUTES = (("x", "z", "y"), ("y", "x", "z"), ("z", "y", "x"))
CAP = 12


def coordinates(index):
    return {
        "z": index // (4 * SIDE * 2),
        "x": lax.rem(index // (2 * SIDE), SIDE),
        "c": lax.rem(index // SIDE, 2),
        "y": lax.rem(index, SIDE),
    }


def place():
    return coordinates(lax.axis_index("blk") * SIDE + lax.axis_index("nb"))


def device(at, **moved):
    to = {**at, **moved}
    return (to["z"] * (2 * SIDE) + to["x"] * 2 + to["c"], to["y"])


def ahead(at, axis, k):
    return lax.rem(at[axis] + (k + SIDE), SIDE)


def meet(partners):
    barrier = pltpu.get_barrier_semaphore()
    for partner in partners:
        pl.semaphore_signal(barrier, inc=1, device_id=partner, device_id_type=MESH)
    pl.semaphore_wait(barrier, len(partners))


class Sender:
    def __init__(self, at, send, recv):
        self.at, self.send, self.recv, self.made = at, send, recv, []

    def push(self, src, dst, **moved):
        n = len(self.made)
        copy = pltpu.make_async_remote_copy(
            src_ref=src, dst_ref=dst, send_sem=self.send.at[n], recv_sem=self.recv.at[n],
            device_id=device(self.at, **moved), device_id_type=MESH,
        )
        self.made.append(copy)
        return copy

    def start(self, src, dst, **moved):
        copy = self.push(src, dst, **moved)
        copy.start()
        return copy

    def finish(self):
        for copy in self.made:
            copy.wait_send()


def everywhere_kernel(x_ref, out_ref, own_sem, send, recv):
    at = place()
    sender = Sender(at, send, recv)
    own = pltpu.make_async_copy(x_ref, out_ref.at[at["z"], at["x"], at["c"], at["y"]], own_sem)
    own.start()
    meet([device(at, **{axis: ahead(at, axis, k)}) for axis in "yxz" for k in (1, 2, 3)] + [device(at, c=1 - at["c"])])
    line = out_ref.at[at["z"], at["x"], at["c"], at["y"]]
    stages = [
        [sender.push(x_ref, line, y=ahead(at, "y", k)) for k in (1, 2, 3)],
        [sender.push(out_ref.at[at["z"], at["x"], at["c"]], out_ref.at[at["z"], at["x"], at["c"]], x=ahead(at, "x", k)) for k in (1, 2, 3)],
        [sender.push(out_ref.at[at["z"], :, at["c"]], out_ref.at[at["z"], :, at["c"]], z=ahead(at, "z", k)) for k in (1, 2, 3)],
        [sender.push(out_ref.at[:, :, at["c"]], out_ref.at[:, :, at["c"]], c=1 - at["c"])],
    ]
    for number, stage in enumerate(stages):
        if number == 1:
            own.wait()
        for copy in stage:
            copy.start()
        for copy in stage:
            copy.wait_recv()
    sender.finish()


def everywhere(x, collective_id):
    out = pl.pallas_call(
        everywhere_kernel,
        out_shape=jax.ShapeDtypeStruct((SIDE, SIDE, 2, SIDE) + x.shape, x.dtype),
        in_specs=[pl.BlockSpec(memory_space=pltpu.VMEM)],
        out_specs=pl.BlockSpec(memory_space=pltpu.VMEM),
        scratch_shapes=[
            pltpu.SemaphoreType.DMA(()),
            pltpu.SemaphoreType.DMA((10,)),
            pltpu.SemaphoreType.DMA((10,)),
        ],
        compiler_params=pltpu.CompilerParams(collective_id=collective_id, has_side_effects=True),
        name="everywhere",
    )(x)
    return out.reshape((2 * SIDE ** 3,) + x.shape)


def deal_kernel(*refs):
    count = len(ROUTES)
    data, got, relay = refs[:count], refs[count:2 * count], refs[2 * count:3 * count]
    own_sem, send, recv = refs[3 * count:]
    at = place()
    c = at["c"]
    half = CAP // 2
    sender = Sender(at, send, recv)
    local = []
    for r, (axis, _, _) in enumerate(ROUTES):
        here = (at[axis], c)
        local.append(pltpu.make_async_copy(data[r].at[here], got[r].at[here], own_sem.at[r]))
        local[-1].start()
    meet(
        [device(at, **{axis: ahead(at, axis, k), "c": cc}) for axis in "xyz" for k in (1, -1) for cc in (0, 1)]
        + [device(at, c=1 - c)]
    )
    relays, plain = [], []
    for r, (axis, _, _) in enumerate(ROUTES):
        far = ahead(at, axis, 2)
        relays.append([
            sender.start(
                data[r].at[far, :, pl.ds(i * half, half)], relay[r].at[i], **{axis: ahead(at, axis, k)}
            )
            for i, k in enumerate((1, -1))
        ])
    for r, (axis, _, _) in enumerate(ROUTES):
        for k in (1, -1):
            to = ahead(at, axis, k)
            for cc in (c, 1 - c):
                plain.append(sender.start(data[r].at[to, cc], got[r].at[at[axis], c], **{axis: to, "c": cc}))
        plain.append(sender.start(data[r].at[at[axis], 1 - c], got[r].at[at[axis], c], c=1 - c))
    for r, (axis, _, _) in enumerate(ROUTES):
        for i, k in enumerate((1, -1)):
            relays[r][i].wait_recv()
            origin = ahead(at, axis, -k)
            for cc in (c, 1 - c):
                plain.append(sender.start(
                    relay[r].at[i, cc], got[r].at[origin, c, pl.ds(i * half, half)],
                    **{axis: ahead(at, axis, k), "c": cc},
                ))
    for copy in plain:
        copy.wait_recv()
    sender.finish()
    for copy in local:
        copy.wait()


def deal(data, collective_id):
    count = len(ROUTES)
    shapes = [jax.ShapeDtypeStruct(a.shape, a.dtype) for a in data]
    copies = (2 + 5 + 4) * count
    rows = data[0].shape[-2]
    return pl.pallas_call(
        deal_kernel,
        out_shape=tuple(shapes),
        in_specs=[pl.BlockSpec(memory_space=pl.ANY)] * count,
        out_specs=(pl.BlockSpec(memory_space=pl.ANY),) * count,
        scratch_shapes=[pltpu.VMEM((2, 2, CAP // 2, rows, 128), jnp.float32)] * count
        + [
            pltpu.SemaphoreType.DMA((count,)),
            pltpu.SemaphoreType.DMA((copies,)),
            pltpu.SemaphoreType.DMA((copies,)),
        ],
        compiler_params=pltpu.CompilerParams(collective_id=collective_id, has_side_effects=True),
        name="deal",
    )(*data)


def pile_kernel(*refs):
    count = len(ROUTES)
    meta, got, dense = refs[0], refs[1:1 + count], refs[1 + count:]
    g = pl.program_id(0)

    @pl.when(g == 0)
    def _():
        for d in dense:
            def clear(i, carry, d=d):
                d[pl.ds(8 * i, 8)] = jnp.zeros((8,) + d.shape[1:], jnp.float32)
                return carry

            lax.fori_loop(0, d.shape[0] // 8, clear, 0)

    for r in range(count):
        def add(i, carry, r=r):
            to = meta[(r * 2 * SIDE + g) * 128 + i]
            dense[r][to] = dense[r][to] + got[r][0, i]
            return carry

        lax.fori_loop(0, meta[(r * 2 * SIDE + g) * 128 + CAP], add, 0)


def pile(meta, got, places):
    count = len(ROUTES)
    rows = got[0].shape[-2]
    slab = pl.BlockSpec((1, CAP, rows, 128), lambda g, *m: (g, 0, 0, 0))
    whole = pl.BlockSpec((places, rows, 128), lambda g, *m: (0, 0, 0))
    return pl.pallas_call(
        pile_kernel,
        out_shape=(jax.ShapeDtypeStruct((places, rows, 128), jnp.float32),) * count,
        grid_spec=pltpu.PrefetchScalarGridSpec(
            num_scalar_prefetch=1,
            grid=(2 * SIDE,),
            in_specs=[slab] * count,
            out_specs=(whole,) * count,
        ),
        compiler_params=pltpu.CompilerParams(vmem_limit_bytes=40 * 1024 * 1024),
        name="pile",
    )(meta, *[a.reshape(2 * SIDE, CAP, rows, 128) for a in got])


def fold_kernel(*refs):
    count = len(ROUTES)
    dense, out, mine = refs[:count], refs[count], refs[count + 1:2 * count + 1]
    passing, direct, second = (refs[(2 + i) * count + 1:(3 + i) * count + 1] for i in range(3))
    own_sem, send, recv = refs[5 * count + 1:]
    at = place()
    sender = Sender(at, send, recv)
    ways = (1, -1)
    cut = (pl.ds(0, 2), pl.ds(2, 2))
    local = []
    for r, (_, f, _) in enumerate(ROUTES):
        local.append([pltpu.make_async_copy(dense[r].at[at[f]], mine[r].at[0], own_sem.at[r, 0])] + [
            pltpu.make_async_copy(dense[r].at[ahead(at, f, k), cut[i]], mine[r].at[1, cut[i]], own_sem.at[r, 1 + i])
            for i, k in enumerate(ways)
        ])
        for copy in local[r]:
            copy.start()
    meet(
        [device(at, **{axis: ahead(at, axis, k)}) for axis in "xyz" for k in (1, 2, 3)]
    )
    ones, straight, twos, threes = [], [], [], []
    for r, (_, f, _) in enumerate(ROUTES):
        ones.append([
            sender.start(dense[r].at[ahead(at, f, 2), cut[i]], passing[r].at[0, cut[i]], **{f: ahead(at, f, k)})
            for i, k in enumerate(ways)
        ])
    for r, (_, f, _) in enumerate(ROUTES):
        straight.append([
            sender.start(dense[r].at[ahead(at, f, k), cut[1 - i]], direct[r].at[cut[1 - i]], **{f: ahead(at, f, k)})
            for i, k in enumerate(ways)
        ])
    for r, (_, f, _) in enumerate(ROUTES):
        twos.append([])
        for i, k in enumerate(ways):
            ones[r][i].wait_recv()
            local[r][1 + i].wait()
            mine[r][1, cut[i]] = mine[r][1, cut[i]] + passing[r][0, cut[i]]
            twos[r].append(sender.start(mine[r].at[1, cut[i]], passing[r].at[1, cut[i]], **{f: ahead(at, f, k)}))
    rows = out.shape[-2] // count
    for r, (_, f, s) in enumerate(ROUTES):
        local[r][0].wait()
        for copy in straight[r] + twos[r]:
            copy.wait_recv()
        mine[r][0] = (mine[r][0] + direct[r][...]) + passing[r][1]
        threes.append([
            sender.start(mine[r].at[0, ahead(at, s, k)], second[r].at[k - 1], **{s: ahead(at, s, k)}) for k in (1, 2, 3)
        ])
    for r, (_, f, s) in enumerate(ROUTES):
        for copy in threes[r]:
            copy.wait_recv()
        out[:, r * rows:(r + 1) * rows, :] = (mine[r][0, at[s]] + second[r][0]) + (second[r][1] + second[r][2])
    sender.finish()


def fold(dense, slots, collective_id):
    count = len(ROUTES)
    rows = dense[0].shape[-2]
    dense = [d.reshape(SIDE, SIDE, slots, rows, 128) for d in dense]
    part = (SIDE, slots, rows, 128)
    copies = (2 + 2 + 2 + 3) * count
    return pl.pallas_call(
        fold_kernel,
        out_shape=jax.ShapeDtypeStruct((slots, count * rows, 128), jnp.float32),
        in_specs=[pl.BlockSpec(memory_space=pl.ANY)] * count,
        out_specs=pl.BlockSpec(memory_space=pltpu.VMEM),
        scratch_shapes=[pltpu.VMEM((2,) + part, jnp.float32)] * count
        + [pltpu.VMEM((2,) + part, jnp.float32)] * count
        + [pltpu.VMEM(part, jnp.float32)] * count
        + [pltpu.VMEM((SIDE - 1,) + part[1:], jnp.float32)] * count
        + [
            pltpu.SemaphoreType.DMA((count, 3)),
            pltpu.SemaphoreType.DMA((copies,)),
            pltpu.SemaphoreType.DMA((copies,)),
        ],
        compiler_params=pltpu.CompilerParams(
            collective_id=collective_id, has_side_effects=True, vmem_limit_bytes=40 * 1024 * 1024
        ),
        name="fold",
    )(*dense)


def apply_kernel(routes, near, *refs):
    pos = refs[1]
    v, refs = refs[2:2 + near], refs[2 + near:]
    own_ref, gh_ref, gl_ref, lh_ref, ll_ref = refs[:5]
    outs, u_ref = refs[5:5 + routes], refs[5 + routes]
    keep, sem = refs[6 + routes:]
    b = pl.program_id(0)
    n = pl.num_programs(0)
    slot = lax.rem(b, 2)
    rows = outs[0].shape[1]

    def copies(b, slot):
        return [
            pltpu.make_async_copy(
                keep.at[slot, k, pl.ds(r * rows, rows)],
                outs[r].at[pos[(r * n + b) * near + k]],
                sem.at[slot, k, r],
            )
            for k in range(near)
            for r in range(routes)
        ]

    values = jnp.concatenate([v[k][0] for k in range(near)], axis=1)
    low = (lh_ref[0], ll_ref[0])
    g = (gh_ref[0], gl_ref[0])
    rest = own_ref[0] - wide(split(values), g, NT)
    u = wide(split(wide(split(rest), low, NT)), low)
    u_ref[0] = u
    pulled = -wide(split(u), g)

    @pl.when(b >= 2)
    def _():
        for copy in copies(b - 2, slot):
            copy.wait()

    for k in range(near):
        keep[slot, k] = pulled[:, k * 128:(k + 1) * 128]
    for copy in copies(b, slot):
        copy.start()

    @pl.when(b == n - 1)
    def _():
        for copy in copies(b - 1, 1 - slot):
            copy.wait()
        for copy in copies(b, slot):
            copy.wait()


def apply_blocks(nbr, positions, length, latent_all, latent, gh, gl, lh, ll):
    n, fields, points = latent.shape
    routes = len(ROUTES)
    near = nbr.shape[1]
    rows = fields // routes

    def v_spec(k):
        return pl.BlockSpec((1, fields, points), lambda b, nbr, pos: (nbr[b * near + k], 0, 0))

    def b_spec(*shape):
        return pl.BlockSpec((1,) + shape, lambda b, nbr, pos: (b, 0, 0))

    return pl.pallas_call(
        functools.partial(apply_kernel, routes, near),
        out_shape=(jax.ShapeDtypeStruct((length, rows, points), jnp.float32),) * routes
        + (jax.ShapeDtypeStruct(latent.shape, jnp.float32),),
        grid_spec=pltpu.PrefetchScalarGridSpec(
            num_scalar_prefetch=2,
            grid=(n,),
            in_specs=[v_spec(k) for k in range(near)]
            + [b_spec(fields, points)]
            + [b_spec(points, near * points)] * 2
            + [b_spec(points, points)] * 2,
            out_specs=(pl.BlockSpec(memory_space=pl.ANY),) * routes + (b_spec(fields, points),),
            scratch_shapes=[
                pltpu.VMEM((2, near, fields, points), jnp.float32),
                pltpu.SemaphoreType.DMA((2, near, routes)),
            ],
        ),
        name="apply",
    )(nbr.reshape(-1), positions, *([latent_all] * near), latent, gh, gl, lh, ll)


def probit_ratio(margin):
    density = jnp.exp(-0.5 * margin * margin - 0.5 * math.log(2.0 * math.pi))
    mass = 0.5 * lax.erfc(-margin / math.sqrt(2.0))
    return density / mass


def rank_of(keys):
    count = keys.shape[-1]
    earlier = lax.broadcasted_iota(jnp.int32, (count, count), 1) < lax.broadcasted_iota(
        jnp.int32, (count, count), 0
    )
    same = keys[..., None, :] == keys[..., :, None]
    return jnp.sum(jnp.where(same & earlier, 1, 0), axis=-1).astype(jnp.int32)


def tables(at, named, places, slots):
    out = []
    for sparse, one, two in ROUTES:
        group_of = []
        for a in range(SIDE):
            for c in range(2):
                blk, nb = device({**at, sparse: a, "c": c})
                group_of.append(blk * SIDE + nb)
        rows = jnp.stack(group_of)
        asked, slot = named[rows], places[rows]
        lies = coordinates(asked)
        mine = (lies[sparse] == at[sparse]) & (lies["c"] == at["c"])
        to = (lies[one] * SIDE + lies[two]) * slots + slot
        keys = jnp.where(mine, 1, 0)
        rank = jnp.where(mine, rank_of(keys), -1)
        lane = lax.broadcasted_iota(jnp.int32, (2 * SIDE, 128, 1), 1)
        meta = jnp.sum(jnp.where(rank[:, None, :] == lane, to[:, None, :], 0), axis=2)
        meta = jnp.where(lane[:, :, 0] == CAP, jnp.sum(keys, axis=1)[:, None], meta)
        out.append(meta.astype(jnp.int32).reshape(-1))
    return jnp.concatenate(out)


def body(latent, coords, labels, owner, slot):
    block_count, field_count, point_count = latent.shape
    near_count = owner.shape[1]
    items = block_count * near_count
    axes = ("blk", "nb")
    device_count = lax.axis_size("blk") * lax.axis_size("nb")
    routes = len(ROUTES)
    rows = field_count // routes
    length = 2 * SIDE * CAP
    at = place()
    wanted = owner.reshape(-1)
    places = slot.reshape(-1)
    lies = coordinates(wanted)
    positions, most = [], 0
    for sparse, _, _ in ROUTES:
        group = lies[sparse] * 2 + lies["c"]
        rank = rank_of(group)
        most = jnp.maximum(most, jnp.max(rank))
        positions.append(group * CAP + jnp.minimum(rank, CAP - 1))
    flag = jnp.where(most >= CAP, 1, 0)
    line = jnp.concatenate([wanted, places, flag[None], jnp.zeros((127 - 2 * items,), jnp.int32)])
    note = jnp.concatenate(
        [
            coords.reshape(2 * block_count, point_count),
            jnp.broadcast_to(line.astype(jnp.float32)[None], (8, point_count)),
        ]
    )
    notes = everywhere(note, 1)
    latent_all = lax.all_gather(latent, axes, axis=0, tiled=True)
    lines = notes[:, 2 * block_count, :].astype(jnp.int32)
    crowded = jnp.max(lines[:, 2 * items]) > 0
    meta = tables(at, lines[:, :items], lines[:, items:2 * items], block_count)
    order = lax.broadcasted_iota(jnp.int32, (items,), 0)
    positions = jnp.concatenate([jnp.where(crowded, order, p) for p in positions])
    capacity = max(2, 2 * items // device_count)

    def requests():
        position = wanted * capacity + rank_of(wanted)
        sent = jnp.full((device_count * capacity,), -1, jnp.int32).at[position].set(places)
        asked = lax.all_to_all(
            sent.reshape(device_count, capacity), axes, split_axis=0, concat_axis=0, tiled=True
        ).reshape(-1)
        return position, asked

    def exchange(x):
        return lax.all_to_all(
            x.reshape(device_count, capacity, field_count, point_count),
            axes, split_axis=0, concat_axis=0, tiled=True,
        ).reshape(device_count * capacity, field_count, point_count)

    gh, gl, lh, ll, qdiag = factor(owner, slot, notes, coords)
    *data, own_part = apply_blocks(
        owner * block_count + slot, positions, length, latent_all, latent, gh, gl, lh, ll
    )

    def routed_return():
        back = deal([d.reshape(SIDE, 2, CAP, rows, point_count) for d in data], 5)
        sums = pile(meta, back, SIDE * SIDE * block_count)
        return fold(sums, block_count, 4)

    def padded_return():
        position, asked = requests()
        near = jnp.concatenate([d[:items] for d in data], axis=1)
        outgoing = jnp.zeros((device_count * capacity, field_count, point_count), jnp.float32)
        returned = exchange(outgoing.at[position].set(near))
        returned = jnp.where((asked >= 0)[:, None, None], returned, 0.0)
        return jnp.zeros_like(latent).at[jnp.maximum(asked, 0)].add(returned)

    prior = own_part + lax.cond(crowded, padded_return, routed_return)
    sign = 2.0 * labels.astype(jnp.float32) - 1.0
    margin = sign * latent
    ratio = probit_ratio(margin)
    weight = ratio * (ratio + margin)
    delta = (sign * ratio - prior) / (weight + qdiag)
    partial = jnp.sum(delta * delta, axis=(0, 2))
    spread = jnp.sum(everywhere(jnp.pad(partial, (0, 128 - field_count))[None], 2), axis=(0, 1))[:field_count]
    step_rms = jnp.sqrt(spread / (block_count * point_count * device_count) + 1e-06)
    new_latent = latent + 0.5 * delta / step_rms[None, :, None]
    return (new_latent, step_rms)


def solution(mesh):
    both = ("blk", "nb")
    return jax.shard_map(
        body,
        mesh=mesh,
        in_specs=(P(both, None, None), P(both, None, None), P(both, None, None), P(both, None), P(both, None)),
        out_specs=(P(both, None, None), P()),
        check_vma=False,
    )
```

profile of v0, /device:TPU:1, one launch (start us, length us, event | category | flops | bytes accessed | tf_op | source)
XLA Modules:
  0.0 253.3 jit_solution(5247276686950500983)
XLA Ops:
  7.2 0.7 all-gather.2.cloned.1.call-update
  8.0 0.8 copy.31.owner_ref
  9.0 0.6 reduce_max.38
  9.9 0.6 reduce_max.36
  11.2 0.6 reduce_max.37
  13.1 0.8 copy.32.slot_ref
  14.0 1.3 pad_maximum_fusion.1.x_ref
  15.3 31.3 %everywhere.2 = f32[4,4,2,4,24,128]{5,4,3,2,1,0:T(8,128)} custom-call(f32[24,128]{1,0:T(8,128)} %pad_maximum_fusion.1.x_ref), custom_call_target="tpu_custom_call" | custom-call | tf_op jit(solution)/shard_map/everywhere/pallas_call | solution.py:283
  46.8 1.1 slice_convert_fusion
  48.0 0.6 gather_fusion.4
  48.5 0.6 gather_fusion.5
  49.2 0.6 gather_fusion
  49.8 0.6 gather_fusion.1
  50.5 0.6 gather_fusion.2
  51.7 0.6 reshape.1551.refs_0_
  52.3 0.7 slice_reduce_fusion
  53.7 0.6 pad_add_fusion.1.refs_1_
  54.8 0.6 select_reduce_fusion.6
  56.1 86.5 %factor.1 = (bf16[8,128,512]{2,1,0:T(8,128)(2,1)}, bf16[8,128,512]{2,1,0:T(8,128)(2,1)}, bf16[8,128,128]{2,1,0:T(8,128)(2,1)}, bf16[8,128,128]{2,1,0:T(8,128)(2,1)}, f32[8,1,128]{2,1,0:T(1,128)}) custom-call(s32[8,4]{1,0:T(8,128)} %copy-done.6, s32[8,4]{1,0:T(8,128)} %copy-done.7, f32[128,24,128]{2,1,0:T(8,128)} %bitcast.69, f32[8,2,128]{2,1,0:T(2,128)} %own_ref.1), custom_call_target="tpu_custom_call" | custom-call | flops 2000000000 | bytes 5000000 | tf_op jit(solution)/shard_map/factor/pallas_call | solution.py:181
  142.6 10.3 %all-gather.2.cloned.1.call-done.refs_2_.refs_3_.refs_4_.refs_5_ = f32[1024,96,128]{2,1,0:T(8,128)} async-done(((f32[8,96,128]{2,1,0:T(8,128)}), f32[1024,96,128]{2,1,0:T(8,128)}) %all-gather.2.cloned.1.call-update) | async-done | bytes 50331664 | tf_op jit(solution)/shard_map/all_gather | solution.py:637
  152.9 12.9 %apply.1 = (f32[96,32,128]{2,1,0:T(8,128)S(1)}, f32[96,32,128]{2,1,0:T(8,128)S(1)}, f32[96,32,128]{2,1,0:T(8,128)}, f32[8,96,128]{2,1,0:T(8,128)}) custom-call(s32[32]{0:T(128)} %reshape.1551.refs_0_, s32[96]{0:T(128)} %pad_add_fusion.1.refs_1_, f32[1024,96,128]{2,1,0:T(8,128)} %all-gather.2.cloned.1.call-done.refs_2_.refs_3_.refs_4_.refs_5_, ...), custom_call_target="tpu_custom_call" | custom-call | tf_op jit(solution)/shard_map/apply/pallas_call | solution.py:551
  165.8 60.3 %conditional.1 = (f32[8,96,128]{2,1,0:T(8,128)}) conditional(s32[]{:T(128)} %convert_element_type.25, (f32[96,32,128]{2,1,0:T(8,128)S(1)}, f32[96,32,128]{2,1,0:T(8,128)S(1)}, f32[96,32,128]{2,1,0:T(8,128)}, s32[3072]{0:T(1024)S(1)}) %tuple.14, (s32[32]{0:T(128)}, s32[8,4]{0,1:T(4,128)S(1)}, s32[8,4]{0,1:T(4,128)}, f32[96,32,128]{2,1,0:T(8,128)S(1)}, ...), branch_computations={%region_16.17_spmd, %region_17.22_spmd} | conditional | flops 7083648 | bytes 124793688 | solution.py:677
  165.8 23.7 %deal.1 = (f32[4,2,12,32,128]{4,3,2,1,0:T(8,128)}, f32[4,2,12,32,128]{4,3,2,1,0:T(8,128)}, f32[4,2,12,32,128]{4,3,2,1,0:T(8,128)}) custom-call(f32[4,2,12,32,128]{4,3,2,1,0:T(8,128)S(1)} %bitcast.65, f32[4,2,12,32,128]{4,3,2,1,0:T(8,128)S(1)} %bitcast.66, f32[4,2,12,32,128]{4,3,2,1,0:T(8,128)} %bitcast.67), custom_call_target="tpu_custom_call" | custom-call | tf_op jit(solution)/shard_map/cond/branch_0_fun/deal/pallas_call | solution.py:352
  189.5 1.4 copy-done
  190.9 1.4 copy-done.1
  192.3 1.4 copy-done.2
  193.7 2.2 pile.1
  196.0 30.0 %fold.1 = f32[8,96,128]{2,1,0:T(8,128)} custom-call(f32[4,4,8,32,128]{4,3,2,1,0:T(8,128)S(1)} %bitcast.58, f32[4,4,8,32,128]{4,3,2,1,0:T(8,128)S(1)} %bitcast.59, f32[4,4,8,32,128]{4,3,2,1,0:T(8,128)S(1)} %bitcast.60), custom_call_target="tpu_custom_call" | custom-call | tf_op jit(solution)/shard_map/cond/branch_0_fun/fold/pallas_call | solution.py:470
  226.1 2.4 multiply_reduce_fusion
  229.0 15.5 %everywhere.3 = f32[4,4,2,4,1,128]{5,4,3,2,1,0:T(1,128)} custom-call(f32[1,128]{1,0:T(1,128)} %pad_bitcast_fusion.x_ref), custom_call_target="tpu_custom_call" | custom-call | tf_op jit(solution)/shard_map/everywhere/pallas_call | solution.py:283
  244.6 1.0 reduce_sum.148
  245.6 0.9 divide_add_fusion
  (62 shorter events, 3.4 us)
Async XLA Ops:
  7.2 44.4 %copy-start.4 = (s32[8,4]{0,1:T(4,128)S(1)}, s32[8,4]{0,1:T(4,128)}, u32[]{:S(2)}) copy-start(s32[8,4]{0,1:T(4,128)} %param.10) | copy-start | bytes 388
  7.2 44.4 %copy-start.5 = (s32[8,4]{0,1:T(4,128)S(1)}, s32[8,4]{0,1:T(4,128)}, u32[]{:S(2)}) copy-start(s32[8,4]{0,1:T(4,128)} %param.11) | copy-start | bytes 388
  7.2 145.7 %all-gather.2.cloned.1.call-start = ((), (), s32[]{:S(2)}) async-start(), calls=%async_computation.2 | async-start | bytes 50724864 | tf_op jit(solution)/shard_map/all_gather | solution.py:637
  8.8 47.3 %copy-start.6 = (s32[8,4]{1,0:T(8,128)}, s32[8,4]{1,0:T(8,128)S(1)}, u32[]{:S(2)}) copy-start(s32[8,4]{1,0:T(8,128)S(1)} %copy.31.owner_ref) | copy-start | bytes 388
  8.8 5.2 %copy-start.8 = (s32[32]{0:T(128)}, s32[32]{0:T(128)S(1)}, u32[]{:S(2)}) copy-start(s32[32]{0:T(128)S(1)} %concatenate.82) | copy-start | bytes 388
  13.9 42.2 %copy-start.7 = (s32[8,4]{1,0:T(8,128)}, s32[8,4]{1,0:T(8,128)S(1)}, u32[]{:S(2)}) copy-start(s32[8,4]{1,0:T(8,128)S(1)} %copy.32.slot_ref) | copy-start | bytes 388
  165.7 60.3 %copy-start.3 = (f32[8,96,128]{2,1,0:T(8,128)S(1)}, f32[8,96,128]{2,1,0:T(8,128)}, u32[]{:S(2)}) copy-start(f32[8,96,128]{2,1,0:T(8,128)} %refs_6_.1) | copy-start | bytes 1179652
  189.5 1.4 copy-start
  190.9 1.4 copy-start.1
  192.3 1.4 copy-start.2
  245.6 0.9 copy-start.9
Sparse Core Ops, SparseCore 0:
  11.0 141.8 all-gather.1
where the time goes:
time: 254 us; the launch traced here: 253 us
  Pallas kernels  202 us (80%)
  between operations  16.9 us (7%)
  other arithmetic  12.2 us (5%)
  waiting for transfers between devices  11 us (4%)
  local copies, waits for them, and re-layouts  10.9 us (4%)
    pallas_call x1, Pallas kernels, factor(): pl.pallas_call(factor_kernel, out_shape=(jax.ShapeDtypeStruct((n, 128, ne...  86.5 us
    pallas_call x2, Pallas kernels, everywhere(): pl.pallas_call(everywhere_kernel, out_shape=jax.ShapeDtypeStruct((SIDE, S...  46.9 us
    pallas_call x1, Pallas kernels, fold(): pl.pallas_call(fold_kernel, out_shape=jax.ShapeDtypeStruct((slots, count...  30 us
    pallas_call x1, Pallas kernels, deal(): pl.pallas_call(deal_kernel, out_shape=tuple(shapes), in_specs=[pl.BlockSp...  23.7 us
    pallas_call x1, Pallas kernels, apply_blocks(): pl.pallas_call(functools.partial(apply_kernel, routes, near), out_shape=(...  12.9 us
    all_gather x1, waiting for transfers between devices, body(): latent_all = lax.all_gather(latent, axes, axis=0, tiled=True)  10.3 us
  transfers between devices with their start and end apart: 1, of which 1 were waited for; matrix products, arithmetic and copies ran while one was open for 6% of the time, Pallas kernels for 47%

commit v1 on v0

--- a/solution.py
+++ b/solution.py
@@ -407,11 +407,12 @@
     )(meta, *[a.reshape(2 * SIDE, CAP, rows, 128) for a in got])
 
 
-def fold_kernel(*refs):
+def fold_kernel(scale, *refs):
     count = len(ROUTES)
-    dense, out, mine = refs[:count], refs[count], refs[count + 1:2 * count + 1]
-    passing, direct, second = (refs[(2 + i) * count + 1:(3 + i) * count + 1] for i in range(3))
-    own_sem, send, recv = refs[5 * count + 1:]
+    dense, (pull_ref, own_ref, weight_ref, latent_ref, new_ref, rms_ref) = refs[:count], refs[count:count + 6]
+    refs = refs[count + 6:]
+    mine, passing, direct, second = (refs[i * count:(i + 1) * count] for i in range(4))
+    delta, line, total, own_sem, line_sem, send, recv = refs[4 * count:]
     at = place()
     sender = Sender(at, send, recv)
     ways = (1, -1)
@@ -425,7 +426,7 @@
         for copy in local[r]:
             copy.start()
     meet(
-        [device(at, **{axis: ahead(at, axis, k)}) for axis in "xyz" for k in (1, 2, 3)]
+        [device(at, **{axis: ahead(at, axis, k)}) for axis in "xyz" for k in (1, 2, 3)] + [device(at, c=1 - at["c"])]
     )
     ones, straight, twos, threes = [], [], [], []
     for r, (_, f, _) in enumerate(ROUTES):
@@ -445,7 +446,7 @@
             local[r][1 + i].wait()
             mine[r][1, cut[i]] = mine[r][1, cut[i]] + passing[r][0, cut[i]]
             twos[r].append(sender.start(mine[r].at[1, cut[i]], passing[r].at[1, cut[i]], **{f: ahead(at, f, k)}))
-    rows = out.shape[-2] // count
+    rows = new_ref.shape[-2] // count
     for r, (_, f, s) in enumerate(ROUTES):
         local[r][0].wait()
         for copy in straight[r] + twos[r]:
@@ -454,30 +455,62 @@
         threes.append([
             sender.start(mine[r].at[0, ahead(at, s, k)], second[r].at[k - 1], **{s: ahead(at, s, k)}) for k in (1, 2, 3)
         ])
+    squares = []
     for r, (_, f, s) in enumerate(ROUTES):
+        part = slice(r * rows, (r + 1) * rows)
+        known = pull_ref[:, part, :] - own_ref[:, part, :]
         for copy in threes[r]:
             copy.wait_recv()
-        out[:, r * rows:(r + 1) * rows, :] = (mine[r][0, at[s]] + second[r][0]) + (second[r][1] + second[r][2])
+        prior = (mine[r][0, at[s]] + second[r][0]) + (second[r][1] + second[r][2])
+        d = (known - prior) / weight_ref[:, part, :]
+        delta[:, part, :] = d
+        squares.append(jnp.sum(d * d, axis=0))
+    squares.append(jnp.zeros((128 - rows * count, 128), jnp.float32))
+    line[...] = jnp.sum(jnp.concatenate(squares, axis=0).T, axis=0, keepdims=True)
+    here = total.at[at["z"], at["x"], at["c"], at["y"]]
+    keep = pltpu.make_async_copy(line, here, line_sem)
+    keep.start()
+    keep.wait()
+    plane, sheet, side = total.at[at["z"], at["x"], at["c"]], total.at[at["z"], :, at["c"]], total.at[:, :, at["c"]]
+    for axis, src in (("y", here), ("x", plane), ("z", sheet)):
+        stage = [sender.start(src, src, **{axis: ahead(at, axis, k)}) for k in (1, 2, 3)]
+        for copy in stage:
+            copy.wait_recv()
+    sender.start(side, side, c=1 - at["c"]).wait_recv()
+    spread = jnp.sum(total[...], axis=(0, 1, 2, 3))
+    rms = jnp.sqrt(spread * scale + 1e-06)
+    rms_ref[...] = rms
+    step = jnp.broadcast_to(0.5 / rms, (128, 128)).T[:rows * count]
+    for b in range(new_ref.shape[0]):
+        new_ref[b] = latent_ref[b] + delta[b] * step
     sender.finish()
 
 
-def fold(dense, slots, collective_id):
+def fold(dense, pull, own_part, weight, latent, points, collective_id):
     count = len(ROUTES)
+    slots = latent.shape[0]
     rows = dense[0].shape[-2]
     dense = [d.reshape(SIDE, SIDE, slots, rows, 128) for d in dense]
     part = (SIDE, slots, rows, 128)
-    copies = (2 + 2 + 2 + 3) * count
+    copies = (2 + 2 + 2 + 3) * count + 10
     return pl.pallas_call(
-        fold_kernel,
-        out_shape=jax.ShapeDtypeStruct((slots, count * rows, 128), jnp.float32),
-        in_specs=[pl.BlockSpec(memory_space=pl.ANY)] * count,
-        out_specs=pl.BlockSpec(memory_space=pltpu.VMEM),
+        functools.partial(fold_kernel, 1.0 / points),
+        out_shape=(
+            jax.ShapeDtypeStruct(latent.shape, jnp.float32),
+            jax.ShapeDtypeStruct((1, 128), jnp.float32),
+        ),
+        in_specs=[pl.BlockSpec(memory_space=pl.ANY)] * count + [pl.BlockSpec(memory_space=pltpu.VMEM)] * 4,
+        out_specs=(pl.BlockSpec(memory_space=pltpu.VMEM),) * 2,
         scratch_shapes=[pltpu.VMEM((2,) + part, jnp.float32)] * count
         + [pltpu.VMEM((2,) + part, jnp.float32)] * count
         + [pltpu.VMEM(part, jnp.float32)] * count
         + [pltpu.VMEM((SIDE - 1,) + part[1:], jnp.float32)] * count
         + [
+            pltpu.VMEM(latent.shape, jnp.float32),
+            pltpu.VMEM((1, 128), jnp.float32),
+            pltpu.VMEM((SIDE, SIDE, 2, SIDE, 1, 128), jnp.float32),
             pltpu.SemaphoreType.DMA((count, 3)),
+            pltpu.SemaphoreType.DMA(()),
             pltpu.SemaphoreType.DMA((copies,)),
             pltpu.SemaphoreType.DMA((copies,)),
         ],
@@ -485,7 +518,7 @@
             collective_id=collective_id, has_side_effects=True, vmem_limit_bytes=40 * 1024 * 1024
         ),
         name="fold",
-    )(*dense)
+    )(*dense, pull, own_part, weight, latent)
 
 
 def apply_kernel(routes, near, *refs):
@@ -661,10 +694,18 @@
         owner * block_count + slot, positions, length, latent_all, latent, gh, gl, lh, ll
     )
 
+    sign = 2.0 * labels.astype(jnp.float32) - 1.0
+    margin = sign * latent
+    ratio = probit_ratio(margin)
+    pull = sign * ratio
+    weight = ratio * (ratio + margin) + qdiag
+    point_total = block_count * point_count * device_count
+
     def routed_return():
         back = deal([d.reshape(SIDE, 2, CAP, rows, point_count) for d in data], 5)
         sums = pile(meta, back, SIDE * SIDE * block_count)
-        return fold(sums, block_count, 4)
+        new_latent, rms = fold(sums, pull, own_part, weight, latent, point_total, 4)
+        return new_latent, rms[0, :field_count]
 
     def padded_return():
         position, asked = requests()
@@ -672,19 +713,14 @@
         outgoing = jnp.zeros((device_count * capacity, field_count, point_count), jnp.float32)
         returned = exchange(outgoing.at[position].set(near))
         returned = jnp.where((asked >= 0)[:, None, None], returned, 0.0)
-        return jnp.zeros_like(latent).at[jnp.maximum(asked, 0)].add(returned)
-
-    prior = own_part + lax.cond(crowded, padded_return, routed_return)
-    sign = 2.0 * labels.astype(jnp.float32) - 1.0
-    margin = sign * latent
-    ratio = probit_ratio(margin)
-    weight = ratio * (ratio + margin)
-    delta = (sign * ratio - prior) / (weight + qdiag)
-    partial = jnp.sum(delta * delta, axis=(0, 2))
-    spread = jnp.sum(everywhere(jnp.pad(partial, (0, 128 - field_count))[None], 2), axis=(0, 1))[:field_count]
-    step_rms = jnp.sqrt(spread / (block_count * point_count * device_count) + 1e-06)
-    new_latent = latent + 0.5 * delta / step_rms[None, :, None]
-    return (new_latent, step_rms)
+        prior = own_part.at[jnp.maximum(asked, 0)].add(returned)
+        delta = (pull - prior) / weight
+        partial = jnp.sum(delta * delta, axis=(0, 2))
+        spread = jnp.sum(everywhere(jnp.pad(partial, (0, 128 - field_count))[None], 2), axis=(0, 1))[:field_count]
+        step_rms = jnp.sqrt(spread / point_total + 1e-06)
+        return latent + 0.5 * delta / step_rms[None, :, None], step_rms
+
+    return lax.cond(crowded, padded_return, routed_return)
 
 
 def solution(mesh):

time: 254 us -> 245 us (0.965)
  Pallas kernels: 202 us -> 197 us
  other arithmetic: 12.2 us -> 9.58 us
    pallas_call x2 -> x1, Pallas kernels: 46.9 us -> 31.3 us  [everywhere(): pl.pallas_call(everywhere_kernel, out_shape=jax.ShapeDtypeStruct((SIDE, S...]
    pallas_call x1, Pallas kernels: 30 us -> 42.3 us  [fold(): pl.pallas_call(functools.partial(fold_kernel, 1.0 / points), out_shape=(j...]
    reduce_sum x2 -> x0, other arithmetic: 3.44 us -> none  [the longest x1 2.44 us: body(): partial = jnp.sum(delta * delta, axis=(0, 2))]
  transfers between devices with their start and end apart: 1 -> 1, of which waited for: 1 -> 1; matrix products, arithmetic and copies ran while one was open for 6% -> 6% of each run, Pallas kernels for 47% -> 48%
where the time goes in v1:
time: 245 us
  Pallas kernels  197 us (80%)
  between operations  16.9 us (7%)
  local copies, waits for them, and re-layouts  11.7 us (5%)
  other arithmetic  9.58 us (4%)
  waiting for transfers between devices  9.12 us (4%)
    pallas_call x1, Pallas kernels, factor(): pl.pallas_call(factor_kernel, out_shape=(jax.ShapeDtypeStruct((n, 128, ne...  86.5 us
    pallas_call x1, Pallas kernels, fold(): pl.pallas_call(functools.partial(fold_kernel, 1.0 / points), out_shape=(j...  42.3 us
    pallas_call x1, Pallas kernels, everywhere(): pl.pallas_call(everywhere_kernel, out_shape=jax.ShapeDtypeStruct((SIDE, S...  31.3 us
    pallas_call x1, Pallas kernels, deal(): pl.pallas_call(deal_kernel, out_shape=tuple(shapes), in_specs=[pl.BlockSp...  24 us
    pallas_call x1, Pallas kernels, apply_blocks(): pl.pallas_call(functools.partial(apply_kernel, routes, near), out_shape=(...  11.2 us
    all_gather x1, waiting for transfers between devices, body(): latent_all = lax.all_gather(latent, axes, axis=0, tiled=True)  8.44 us
  transfers between devices with their start and end apart: 1, of which 1 were waited for; matrix products, arithmetic and copies ran while one was open for 6% of the time, Pallas kernels for 48%

profile of v1, /device:TPU:1, one launch (start us, length us, event | category | flops | bytes accessed | tf_op | source)
XLA Modules:
  0.0 244.9 jit_solution(3001252593252014320)
XLA Ops:
  7.2 0.7 all-gather.2.cloned.1.call-update
  8.0 0.8 copy.32.owner_ref
  9.0 0.6 reduce_max.38
  9.9 0.6 reduce_max.36
  11.2 0.6 reduce_max.37
  13.1 0.8 copy.33.slot_ref
  14.0 1.3 pad_maximum_fusion.1.x_ref
  15.3 31.3 %everywhere.3 = f32[4,4,2,4,24,128]{5,4,3,2,1,0:T(8,128)} custom-call(f32[24,128]{1,0:T(8,128)} %pad_maximum_fusion.1.x_ref), custom_call_target="tpu_custom_call" | custom-call | tf_op jit(solution)/shard_map/everywhere/pallas_call | solution.py:283
  46.8 1.1 slice_convert_fusion
  48.0 0.6 gather_fusion.4
  48.5 0.6 gather_fusion.5
  49.2 0.6 gather_fusion
  49.8 0.6 gather_fusion.1
  50.5 0.6 gather_fusion.2
  51.0 0.6 gather_fusion.3
  51.7 0.6 reshape.1553.refs_0_
  52.4 0.7 slice_reduce_fusion
  53.8 0.6 pad_add_fusion.1.refs_1_
  54.8 0.6 select_reduce_fusion.6
  56.1 86.5 %factor.1 = (bf16[8,128,512]{2,1,0:T(8,128)(2,1)}, bf16[8,128,512]{2,1,0:T(8,128)(2,1)}, bf16[8,128,128]{2,1,0:T(8,128)(2,1)}, bf16[8,128,128]{2,1,0:T(8,128)(2,1)}, f32[8,1,128]{2,1,0:T(1,128)}) custom-call(s32[8,4]{1,0:T(8,128)} %copy-done.7, s32[8,4]{1,0:T(8,128)} %copy-done.8, f32[128,24,128]{2,1,0:T(8,128)} %bitcast.71, f32[8,2,128]{2,1,0:T(2,128)} %own_ref.1), custom_call_target="tpu_custom_call" | custom-call | flops 2000000000 | bytes 5000000 | tf_op jit(solution)/shard_map/factor/pallas_call | solution.py:181
  142.7 1.7 fusion.8
  144.4 8.4 %all-gather.2.cloned.1.call-done.refs_2_.refs_3_.refs_4_.refs_5_ = f32[1024,96,128]{2,1,0:T(8,128)} async-done(((f32[8,96,128]{2,1,0:T(8,128)}), f32[1024,96,128]{2,1,0:T(8,128)}) %all-gather.2.cloned.1.call-update) | async-done | bytes 50331664 | tf_op jit(solution)/shard_map/all_gather | solution.py:670
  152.8 11.2 %apply.1 = (f32[96,32,128]{2,1,0:T(8,128)S(1)}, f32[96,32,128]{2,1,0:T(8,128)}, f32[96,32,128]{2,1,0:T(8,128)}, f32[8,96,128]{2,1,0:T(8,128)S(1)}) custom-call(s32[32]{0:T(128)} %reshape.1553.refs_0_, s32[96]{0:T(128)} %pad_add_fusion.1.refs_1_, f32[1024,96,128]{2,1,0:T(8,128)} %all-gather.2.cloned.1.call-done.refs_2_.refs_3_.refs_4_.refs_5_, ...), custom_call_target="tpu_custom_call" | custom-call | tf_op jit(solution)/shard_map/apply/pallas_call | solution.py:584
  164.1 73.2 %conditional.1 = (f32[8,96,128]{2,1,0:T(8,128)S(1)}, f32[96]{0:T(128)}) conditional(s32[]{:T(128)} %convert_element_type.24, (f32[96,32,128]{2,1,0:T(8,128)S(1)}, f32[96,32,128]{2,1,0:T(8,128)}, f32[96,32,128]{2,1,0:T(8,128)}, s32[3072]{0:T(1024)S(1)}, f32[8,96,128]{2,1,0:T(8,128)S(1)}, /*index=5*/f32[8,96,128]{2,1,0:T(8,128)S(1)}, ...), branch_computations={%region_16.17_spmd, %region_17.24_spmd} | conditional | flops 7788128 | bytes 127221472 | solution.py:723
  164.1 24.0 %deal.1 = (f32[4,2,12,32,128]{4,3,2,1,0:T(8,128)}, f32[4,2,12,32,128]{4,3,2,1,0:T(8,128)}, f32[4,2,12,32,128]{4,3,2,1,0:T(8,128)}) custom-call(f32[4,2,12,32,128]{4,3,2,1,0:T(8,128)S(1)} %bitcast.67, f32[4,2,12,32,128]{4,3,2,1,0:T(8,128)} %bitcast.68, f32[4,2,12,32,128]{4,3,2,1,0:T(8,128)} %bitcast.69), custom_call_target="tpu_custom_call" | custom-call | tf_op jit(solution)/shard_map/cond/branch_0_fun/deal/pallas_call | solution.py:352
  188.1 1.4 copy-done
  189.5 1.4 copy-done.1
  190.9 1.4 copy-done.2
  192.3 2.1 pile.1
  194.4 42.3 %fold.1 = (f32[8,96,128]{2,1,0:T(8,128)S(1)}, f32[1,128]{1,0:T(1,128)S(1)}) custom-call(f32[4,4,8,32,128]{4,3,2,1,0:T(8,128)S(1)} %bitcast.60, f32[4,4,8,32,128]{4,3,2,1,0:T(8,128)S(1)} %bitcast.61, f32[4,4,8,32,128]{4,3,2,1,0:T(8,128)S(1)} %bitcast.62, f32[8,96,128]{2,1,0:T(8,128)S(1)} %get-tuple-element.47.refs_3_, ...), custom_call_target="tpu_custom_call" | custom-call | tf_op jit(solution)/shard_map/cond/branch_0_fun/fold/pallas_call | solution.py:496
  236.8 0.5 slice_bitcast_fusion
  237.3 0.7 copy.46
  (58 shorter events, 2.4 us)
Async XLA Ops:
  7.2 44.4 %copy-start.5 = (s32[8,4]{0,1:T(4,128)S(1)}, s32[8,4]{0,1:T(4,128)}, u32[]{:S(2)}) copy-start(s32[8,4]{0,1:T(4,128)} %param.10) | copy-start | bytes 388
  7.2 44.4 %copy-start.6 = (s32[8,4]{0,1:T(4,128)S(1)}, s32[8,4]{0,1:T(4,128)}, u32[]{:S(2)}) copy-start(s32[8,4]{0,1:T(4,128)} %param.11) | copy-start | bytes 388
  7.2 145.7 %all-gather.2.cloned.1.call-start = ((), (), s32[]{:S(2)}) async-start(), calls=%async_computation.2 | async-start | bytes 50724864 | tf_op jit(solution)/shard_map/all_gather | solution.py:670
  8.8 47.4 %copy-start.7 = (s32[8,4]{1,0:T(8,128)}, s32[8,4]{1,0:T(8,128)S(1)}, u32[]{:S(2)}) copy-start(s32[8,4]{1,0:T(8,128)S(1)} %copy.32.owner_ref) | copy-start | bytes 388
  13.9 42.2 %copy-start.8 = (s32[8,4]{1,0:T(8,128)}, s32[8,4]{1,0:T(8,128)S(1)}, u32[]{:S(2)}) copy-start(s32[8,4]{1,0:T(8,128)S(1)} %copy.33.slot_ref) | copy-start | bytes 388
  56.1 86.5 %copy-start.3 = (f32[8,96,128]{2,1,0:T(8,128)S(1)}, f32[8,96,128]{2,1,0:T(8,128)}, u32[]{:S(2)}) copy-start(f32[8,96,128]{2,1,0:T(8,128)} %refs_6_.1) | copy-start | bytes 1179652
  56.1 86.5 %copy-start.4 = (s32[8,96,128]{2,1,0:T(8,128)S(1)}, s32[8,96,128]{2,1,0:T(8,128)}, u32[]{:S(2)}) copy-start(s32[8,96,128]{2,1,0:T(8,128)} %param.9) | copy-start | bytes 1179652
  188.1 1.4 copy-start
  189.5 1.4 copy-start.1
  190.9 1.4 copy-start.2
Sparse Core Ops, SparseCore 0:
  11.0 141.7 all-gather.1

commit v2 on v1

--- a/solution.py
+++ b/solution.py
@@ -402,7 +402,7 @@
             in_specs=[slab] * count,
             out_specs=(whole,) * count,
         ),
-        compiler_params=pltpu.CompilerParams(vmem_limit_bytes=40 * 1024 * 1024),
+        compiler_params=pltpu.CompilerParams(vmem_limit_bytes=54 * 1024 * 1024),
         name="pile",
     )(meta, *[a.reshape(2 * SIDE, CAP, rows, 128) for a in got])
 

time: 245 us -> 252 us (1.029)
  Pallas kernels: 197 us -> 204 us
    pallas_call x1, Pallas kernels: 2.14 us -> 8.79 us  [pile(): pl.pallas_call(pile_kernel, out_shape=(jax.ShapeDtypeStruct((places, rows...]
  transfers between devices with their start and end apart: 1 -> 1, of which waited for: 1 -> 1; matrix products, arithmetic and copies ran while one was open for 6% -> 6% of each run, Pallas kernels for 48% -> 47%
where the time goes in v2:
time: 252 us
  Pallas kernels  204 us (81%)
  between operations  16.9 us (7%)
  local copies, waits for them, and re-layouts  12.2 us (5%)
  other arithmetic  9.58 us (4%)
  waiting for transfers between devices  9.12 us (4%)
    pallas_call x1, Pallas kernels, factor(): pl.pallas_call(factor_kernel, out_shape=(jax.ShapeDtypeStruct((n, 128, ne...  86.5 us
    pallas_call x1, Pallas kernels, fold(): pl.pallas_call(functools.partial(fold_kernel, 1.0 / points), out_shape=(j...  42.1 us
    pallas_call x1, Pallas kernels, everywhere(): pl.pallas_call(everywhere_kernel, out_shape=jax.ShapeDtypeStruct((SIDE, S...  31.3 us
    pallas_call x1, Pallas kernels, deal(): pl.pallas_call(deal_kernel, out_shape=tuple(shapes), in_specs=[pl.BlockSp...  24 us
    pallas_call x1, Pallas kernels, apply_blocks(): pl.pallas_call(functools.partial(apply_kernel, routes, near), out_shape=(...  11.2 us
    pallas_call x1, Pallas kernels, pile(): pl.pallas_call(pile_kernel, out_shape=(jax.ShapeDtypeStruct((places, rows...  8.79 us
    all_gather x1, waiting for transfers between devices, body(): latent_all = lax.all_gather(latent, axes, axis=0, tiled=True)  8.44 us
  transfers between devices with their start and end apart: 1, of which 1 were waited for; matrix products, arithmetic and copies ran while one was open for 6% of the time, Pallas kernels for 47%

profile of v2, /device:TPU:1, one launch (start us, length us, event | category | flops | bytes accessed | tf_op | source)
XLA Modules:
  0.0 251.8 jit_solution(13957372017309730027)
XLA Ops:
  7.2 0.7 all-gather.2.cloned.1.call-update
  8.0 0.8 copy.32.owner_ref
  9.0 0.6 reduce_max.38
  9.9 0.6 reduce_max.36
  11.2 0.6 reduce_max.37
  13.1 0.8 copy.33.slot_ref
  14.0 1.3 pad_maximum_fusion.1.x_ref
  15.3 31.3 %everywhere.3 = f32[4,4,2,4,24,128]{5,4,3,2,1,0:T(8,128)} custom-call(f32[24,128]{1,0:T(8,128)} %pad_maximum_fusion.1.x_ref), custom_call_target="tpu_custom_call" | custom-call | tf_op jit(solution)/shard_map/everywhere/pallas_call | solution.py:283
  46.8 1.1 slice_convert_fusion
  48.0 0.6 gather_fusion.4
  48.5 0.6 gather_fusion.5
  49.2 0.6 gather_fusion
  49.8 0.6 gather_fusion.1
  50.5 0.6 gather_fusion.2
  51.0 0.6 gather_fusion.3
  51.7 0.6 reshape.1553.refs_0_
  52.4 0.7 slice_reduce_fusion
  53.8 0.6 pad_add_fusion.1.refs_1_
  54.8 0.6 select_reduce_fusion.6
  56.1 86.5 %factor.1 = (bf16[8,128,512]{2,1,0:T(8,128)(2,1)}, bf16[8,128,512]{2,1,0:T(8,128)(2,1)}, bf16[8,128,128]{2,1,0:T(8,128)(2,1)}, bf16[8,128,128]{2,1,0:T(8,128)(2,1)}, f32[8,1,128]{2,1,0:T(1,128)}) custom-call(s32[8,4]{1,0:T(8,128)} %copy-done.7, s32[8,4]{1,0:T(8,128)} %copy-done.8, f32[128,24,128]{2,1,0:T(8,128)} %bitcast.68, f32[8,2,128]{2,1,0:T(2,128)} %own_ref.1), custom_call_target="tpu_custom_call" | custom-call | flops 2000000000 | bytes 5000000 | tf_op jit(solution)/shard_map/factor/pallas_call | solution.py:181
  142.7 1.7 fusion.8
  144.4 8.4 %all-gather.2.cloned.1.call-done.refs_2_.refs_3_.refs_4_.refs_5_ = f32[1024,96,128]{2,1,0:T(8,128)} async-done(((f32[8,96,128]{2,1,0:T(8,128)}), f32[1024,96,128]{2,1,0:T(8,128)}) %all-gather.2.cloned.1.call-update) | async-done | bytes 50331664 | tf_op jit(solution)/shard_map/all_gather | solution.py:670
  152.8 11.2 %apply.1 = (f32[96,32,128]{2,1,0:T(8,128)S(1)}, f32[96,32,128]{2,1,0:T(8,128)}, f32[96,32,128]{2,1,0:T(8,128)}, f32[8,96,128]{2,1,0:T(8,128)S(1)}) custom-call(s32[32]{0:T(128)} %reshape.1553.refs_0_, s32[96]{0:T(128)} %pad_add_fusion.1.refs_1_, f32[1024,96,128]{2,1,0:T(8,128)} %all-gather.2.cloned.1.call-done.refs_2_.refs_3_.refs_4_.refs_5_, ...), custom_call_target="tpu_custom_call" | custom-call | tf_op jit(solution)/shard_map/apply/pallas_call | solution.py:584
  164.1 80.1 %conditional.1 = (f32[8,96,128]{2,1,0:T(8,128)S(1)}, f32[96]{0:T(128)}) conditional(s32[]{:T(128)} %convert_element_type.24, (f32[96,32,128]{2,1,0:T(8,128)S(1)}, f32[96,32,128]{2,1,0:T(8,128)}, f32[96,32,128]{2,1,0:T(8,128)}, s32[3072]{0:T(1024)S(1)}, f32[8,96,128]{2,1,0:T(8,128)S(1)}, /*index=5*/f32[8,96,128]{2,1,0:T(8,128)S(1)}, ...), branch_computations={%region_16.17_spmd, %region_17.24_spmd} | conditional | flops 7788128 | bytes 127221472 | solution.py:723
  164.1 24.0 %deal.1 = (f32[4,2,12,32,128]{4,3,2,1,0:T(8,128)}, f32[4,2,12,32,128]{4,3,2,1,0:T(8,128)}, f32[4,2,12,32,128]{4,3,2,1,0:T(8,128)}) custom-call(f32[4,2,12,32,128]{4,3,2,1,0:T(8,128)S(1)} %bitcast.64, f32[4,2,12,32,128]{4,3,2,1,0:T(8,128)} %bitcast.65, f32[4,2,12,32,128]{4,3,2,1,0:T(8,128)} %bitcast.66), custom_call_target="tpu_custom_call" | custom-call | tf_op jit(solution)/shard_map/cond/branch_0_fun/deal/pallas_call | solution.py:352
  188.1 8.8 %pile.1 = (f32[128,32,128]{2,1,0:T(8,128)}, f32[128,32,128]{2,1,0:T(8,128)}, f32[128,32,128]{2,1,0:T(8,128)}) custom-call(s32[3072]{0:T(1024)S(1)} %get-tuple-element.37.refs_0_, f32[8,12,32,128]{3,2,1,0:T(8,128)} %bitcast.69, f32[8,12,32,128]{3,2,1,0:T(8,128)} %bitcast.70, f32[8,12,32,128]{3,2,1,0:T(8,128)} %bitcast.71), custom_call_target="tpu_custom_call" | custom-call | tf_op jit(solution)/shard_map/cond/branch_0_fun/pile/pallas_call | solution.py:396
  196.9 1.6 copy-done
  198.5 1.6 copy-done.1
  200.0 1.6 copy-done.2
  201.6 42.1 %fold.1 = (f32[8,96,128]{2,1,0:T(8,128)S(1)}, f32[1,128]{1,0:T(1,128)S(1)}) custom-call(f32[4,4,8,32,128]{4,3,2,1,0:T(8,128)S(1)} %bitcast.60, f32[4,4,8,32,128]{4,3,2,1,0:T(8,128)S(1)} %bitcast.61, f32[4,4,8,32,128]{4,3,2,1,0:T(8,128)S(1)} %bitcast.62, f32[8,96,128]{2,1,0:T(8,128)S(1)} %get-tuple-element.47.refs_3_, ...), custom_call_target="tpu_custom_call" | custom-call | tf_op jit(solution)/shard_map/cond/branch_0_fun/fold/pallas_call | solution.py:496
  243.7 0.5 slice_bitcast_fusion
  244.2 0.7 copy.46
  (58 shorter events, 2.4 us)
Async XLA Ops:
  7.2 44.4 %copy-start.5 = (s32[8,4]{0,1:T(4,128)S(1)}, s32[8,4]{0,1:T(4,128)}, u32[]{:S(2)}) copy-start(s32[8,4]{0,1:T(4,128)} %param.10) | copy-start | bytes 388
  7.2 44.4 %copy-start.6 = (s32[8,4]{0,1:T(4,128)S(1)}, s32[8,4]{0,1:T(4,128)}, u32[]{:S(2)}) copy-start(s32[8,4]{0,1:T(4,128)} %param.11) | copy-start | bytes 388
  7.2 145.7 %all-gather.2.cloned.1.call-start = ((), (), s32[]{:S(2)}) async-start(), calls=%async_computation.2 | async-start | bytes 50724864 | tf_op jit(solution)/shard_map/all_gather | solution.py:670
  8.8 47.4 %copy-start.7 = (s32[8,4]{1,0:T(8,128)}, s32[8,4]{1,0:T(8,128)S(1)}, u32[]{:S(2)}) copy-start(s32[8,4]{1,0:T(8,128)S(1)} %copy.32.owner_ref) | copy-start | bytes 388
  13.9 42.2 %copy-start.8 = (s32[8,4]{1,0:T(8,128)}, s32[8,4]{1,0:T(8,128)S(1)}, u32[]{:S(2)}) copy-start(s32[8,4]{1,0:T(8,128)S(1)} %copy.33.slot_ref) | copy-start | bytes 388
  56.1 86.5 %copy-start.3 = (f32[8,96,128]{2,1,0:T(8,128)S(1)}, f32[8,96,128]{2,1,0:T(8,128)}, u32[]{:S(2)}) copy-start(f32[8,96,128]{2,1,0:T(8,128)} %refs_6_.1) | copy-start | bytes 1179652
  56.1 86.5 %copy-start.4 = (s32[8,96,128]{2,1,0:T(8,128)S(1)}, s32[8,96,128]{2,1,0:T(8,128)}, u32[]{:S(2)}) copy-start(s32[8,96,128]{2,1,0:T(8,128)} %param.9) | copy-start | bytes 1179652
  196.9 1.6 copy-start
  198.5 1.6 copy-start.1
  200.0 1.6 copy-start.2
Sparse Core Ops, SparseCore 0:
  11.0 141.7 all-gather.1
